TPU v7x, 32 devices: a whole 2x2x4 slice. The times are simulated.
32 devices in a mesh: groups: 2 (over y), dp: 4 (over x, core), tensor: 4 (over z).
Axes of the slice: x: 2, y: 2, z: 4, core: 2. Of those that a mesh axis runs over, the one named last changes fastest.
Arguments:
- query: bfloat16 [4096, 512], P(('groups', 'dp'), 'tensor'), parts along dimension 0, may hold values from -4.5 to 4.5
- keys: bfloat16 [4096, 512], P(('groups', 'dp'), 'tensor'), parts along dimension 0, may hold values from -4.5 to 4.5
- values: bfloat16 [4096, 512], P(('groups', 'dp'), 'tensor'), parts along dimension 0, may hold values from -6 to 6
- upstream: bfloat16 [4096, 8192], P(('groups', 'dp', 'tensor')), parts along dimension 0, may hold values from -6 to 6
- projection: bfloat16 [512, 8192], P('tensor', 'dp'), may hold values from -0.0625 to 0.0625
- lengths: int32 [8, 8], P(('groups', 'dp')), parts along dimension 0, may hold values from 1 to 256, 512 in all within a row
Outputs:
- grad_query: bfloat16 [4096, 512], P(('groups', 'dp'), 'tensor'), parts along dimension 0
- grad_keys: bfloat16 [4096, 512], P(('groups', 'dp'), 'tensor'), parts along dimension 0
- grad_values: bfloat16 [4096, 512], P(('groups', 'dp'), 'tensor'), parts along dimension 0
- grad_projection: float32 [1024, 8192], P(('groups', 'tensor'), 'dp'), parts along dimension 0
There are 2 independent parts, one for each index of `groups`. A program takes and returns all parts, laid end to end along the dimension named above; an argument that names none is the same for every part. Nothing has to cross between parts.
Inputs may be any that keep to these rules, and one draw needn't show every extreme that they name: Each row holds the lengths of the 8 documents of one sequence in order; they sum to 512 and the largest is exactly 256.
All inputs are finite; a program needn't handle non-finite values.
Results may differ from a plain program's by a relative error of at most 0.014.
Values may be sent and summed in bfloat16 or wider, within the bound.
No kernel may reach another device: no remote copies, remote signals or barrier semaphores. Data moves between devices by JAX's collectives and lax.ppermute only.
A program may use at most 64 MiB of HBM per device.

v0:
```python
import jax
import jax.numpy as jnp
from jax import lax
from jax.sharding import PartitionSpec as P

HD = 128


def sequence_mask(length_row, row_count):
    segment_ends = jnp.cumsum(length_row)
    places = jnp.arange(row_count, dtype=jnp.int32)
    labels = jnp.sum((segment_ends[None, :] <= places[:, None]).astype(jnp.int32), axis=1)
    same = labels[:, None] == labels[None, :]
    return jnp.logical_and(same, places[None, :] <= places[:, None])


def shards(query, keys, values, upstream, projection, lengths):
    row_count, width = query.shape
    head_count = width // HD
    scaling = HD ** (-0.5)
    allowed = sequence_mask(lengths[0], row_count)
    query_heads = query.reshape(row_count, head_count, HD)
    key_heads = keys.reshape(row_count, head_count, HD)
    value_heads = values.reshape(row_count, head_count, HD)
    scores = (
        jnp.einsum("qhd,khd->hqk", query_heads, key_heads, preferred_element_type=jnp.float32)
        * scaling
    )
    scores = jnp.where(allowed[None], scores, -1e30)
    row_max = jnp.max(scores, axis=2, keepdims=True)
    exponent = jnp.exp(scores - row_max)
    probs = exponent / jnp.sum(exponent, axis=2, keepdims=True)
    probs_low = probs.astype(jnp.bfloat16)
    attended = jnp.einsum(
        "hqk,khd->qhd", probs_low, value_heads, preferred_element_type=jnp.float32
    )
    attended = attended.astype(jnp.bfloat16).reshape(row_count, width)
    full_projection = lax.all_gather(projection, "dp", axis=1, tiled=True)
    gathered = lax.all_gather(upstream, "tensor", axis=0, tiled=True)
    out_total = lax.dot_general(
        gathered, full_projection, (((1,), (1,)), ((), ())), preferred_element_type=jnp.float32
    )
    partial_grad = lax.dot_general(
        attended, gathered, (((0,), (0,)), ((), ())), preferred_element_type=jnp.float32
    )
    grad_projection = lax.psum_scatter(
        partial_grad.astype(jnp.bfloat16), "dp", scatter_dimension=1, tiled=True
    ).astype(jnp.float32)
    out_grad = out_total.astype(jnp.bfloat16)
    grad_heads = out_grad.reshape(row_count, head_count, HD)
    grad_values = jnp.einsum(
        "hqk,qhd->khd", probs_low, grad_heads, preferred_element_type=jnp.float32
    ).astype(jnp.bfloat16)
    grad_probs = jnp.einsum(
        "qhd,khd->hqk", grad_heads, value_heads, preferred_element_type=jnp.float32
    )
    delta = jnp.sum(probs * grad_probs, axis=2, keepdims=True)
    grad_scores = (probs * (grad_probs - delta) * scaling).astype(jnp.bfloat16)
    grad_query = jnp.einsum(
        "hqk,khd->qhd", grad_scores, key_heads, preferred_element_type=jnp.float32
    ).astype(jnp.bfloat16)
    grad_keys = jnp.einsum(
        "hqk,qhd->khd", grad_scores, query_heads, preferred_element_type=jnp.float32
    ).astype(jnp.bfloat16)
    return (
        grad_query.reshape(row_count, width),
        grad_keys.reshape(row_count, width),
        grad_values.reshape(row_count, width),
        grad_projection,
    )


def solution(mesh):
    in_specs = (
        P(("groups", "dp"), "tensor"),
        P(("groups", "dp"), "tensor"),
        P(("groups", "dp"), "tensor"),
        P(("groups", "dp", "tensor"), None),
        P("tensor", "dp"),
        P(("groups", "dp"), None),
    )
    out_specs = (
        P(("groups", "dp"), "tensor"),
        P(("groups", "dp"), "tensor"),
        P(("groups", "dp"), "tensor"),
        P(("groups", "tensor"), "dp"),
    )
    return jax.shard_map(shards, mesh=mesh, in_specs=in_specs, out_specs=out_specs, check_vma=False)
```

profile of v0, /device:TPU:0, one launch (start us, length us, event | category | flops | bytes accessed | tf_op | source)
XLA Modules:
  0.0 226.7 jit_solution(17024745603641305551)
XLA Ops:
  7.2 0.0 copy-start
  7.2 0.0 all-gather.3.cloned.1.call-start
  7.2 0.7 all-gather.3.cloned.1.call-update
  7.9 0.0 all-gather.5.cloned.1.call-start
  8.0 0.7 all-gather.5.cloned.1.call-update
  8.7 0.0 reduce-scatter.2.cloned.1.call-start
  8.7 0.8 reduce-window.8
  9.5 0.1 convert_reduce_fusion
  9.6 1.3 fusion.11
  10.9 0.2 fusion.4
  11.1 150.8 %all-gather.3.cloned.1.call-done = bf16[512,8192]{1,0:T(8,128)(2,1)} async-done(((bf16[128,8192]{1,0:T(8,128)(2,1)}), bf16[512,8192]{1,0:T(8,128)(2,1)}) %all-gather.3.cloned.1.call-update) | async-done | bytes 8388624 | tf_op jit(solution)/shard_map/all_gather | solution.py:39
  161.9 6.5 %convolution_convert_fusion = bf16[128,8192]{1,0:T(8,128)(2,1)} fusion(bf16[512,8192]{1,0:T(8,128)(2,1)} %all-gather.3.cloned.1.call-done, bf16[512,128]{1,0:T(8,128)(2,1)S(1)} %copy-done, f32[512,512]{0,1:T(8,128)S(1)} %get-tuple-element.13, f32[512]{0:T(512)S(1)} %fusion.4, f32[512]{0:T(512)S(1)} %get-tuple-element.12), kind=kOutput, calls=%fused_computation | convolution fusion | flops 1142751232 | bytes 11669504 | tf_op jit(solution)/shard_map/dot_general | solution.py:43
  168.4 0.0 reduce-scatter.2.cloned.1.call-update
  168.4 15.8 %all-gather.5.cloned.1.call-done = bf16[128,8192]{1,0:T(8,128)(2,1)} async-done(((bf16[128,2048]{1,0:T(8,128)(2,1)}), bf16[128,8192]{1,0:T(8,128)(2,1)}) %all-gather.5.cloned.1.call-update) | async-done | bytes 2097168 | tf_op jit(solution)/shard_map/all_gather | solution.py:38
  184.3 6.3 %convolution_convert_fusion.5 = bf16[512,128]{1,0:T(8,128)(2,1)S(1)} fusion(bf16[512,8192]{1,0:T(8,128)(2,1)} %all-gather.3.cloned.1.call-done, bf16[128,8192]{1,0:T(8,128)(2,1)} %all-gather.5.cloned.1.call-done), kind=kOutput, calls=%fused_computation.7 | convolution fusion | flops 1073807360 | bytes 10616832 | tf_op jit(solution)/shard_map/dot_general | solution.py:40
  190.6 0.3 fusion.1
  190.9 0.0 copy-start.2
  191.0 0.8 copy.11
  191.7 0.3 multiply_reduce_fusion
  192.0 0.3 multiply_convert_fusion
  192.3 1.0 convolution_convert_fusion.3
  193.3 1.0 convolution_convert_fusion.4
  194.3 23.7 %reduce-scatter.2.cloned.1.call-done = bf16[128,2048]{1,0:T(8,128)(2,1)} async-done(((bf16[128,8192]{1,0:T(8,128)(2,1)}), bf16[128,2048]{1,0:T(8,128)(2,1)}) %reduce-scatter.2.cloned.1.call-update) | async-done | bytes 524304 | tf_op jit(solution)/shard_map/reduce_scatter | solution.py:46
  218.0 2.1 convert_element_type.58
  (4 shorter events, 0.0 us)
Async XLA Ops:
  7.2 154.8 %copy-start = (bf16[512,128]{1,0:T(8,128)(2,1)S(1)}, bf16[512,128]{1,0:T(8,128)(2,1)}, u32[]{:S(2)}) copy-start(bf16[512,128]{1,0:T(8,128)(2,1)} %param.8) | copy-start | bytes 393220
  7.2 154.7 %all-gather.3.cloned.1.call-start = ((), (), s32[]{:S(2)}) async-start(), calls=%async_computation.1 | async-start | bytes 10485760 | tf_op jit(solution)/shard_map/all_gather | solution.py:39
  7.9 176.4 %all-gather.5.cloned.1.call-start = ((), (), s32[]{:S(2)}) async-start(), calls=%async_computation.2 | async-start | bytes 2621440 | tf_op jit(solution)/shard_map/all_gather | solution.py:38
  8.7 209.3 %reduce-scatter.2.cloned.1.call-start = ((), (), s32[]{:S(2)}) async-start(), calls=%async_computation.3 | async-start | bytes 2621440 | tf_op jit(solution)/shard_map/reduce_scatter | solution.py:46
  190.9 1.4 copy-start.1
  190.9 2.4 %copy-start.2 = (bf16[512,128]{1,0:T(8,128)(2,1)S(1)}, bf16[512,128]{1,0:T(8,128)(2,1)}, u32[]{:S(2)}) copy-start(bf16[512,128]{1,0:T(8,128)(2,1)} %param.7) | copy-start | bytes 393220
Sparse Core Ops, SparseCore 0:
  9.6 152.3 all-gather.2
  163.5 20.7 all-gather.4
  186.8 31.1 reduce-scatter.1
where the time goes:
time: 227 us
  waiting for transfers between devices  192 us (85%)
  matrix products  16.7 us (7%)
  between operations  13.8 us (6%)
  other arithmetic  3.53 us (2%)
    all_gather x1, waiting for transfers between devices, shards(): gathered = lax.all_gather(upstream, 'tensor', axis=0, tiled=True)  151 us
    reduce_scatter x1, waiting for transfers between devices, shards(): lax.psum_scatter(partial_grad.astype(jnp.bfloat16), 'dp', scatter_dimensi...  23.7 us
    all_gather x1, waiting for transfers between devices, shards(): full_projection = lax.all_gather(projection, 'dp', axis=1, tiled=True)  15.8 us
    dot_general x1, matrix products, shards(): lax.dot_general(attended, gathered, (((0,), (0,)), ((), ())), preferred_e...  6.48 us
    dot_general x1, matrix products, shards(): lax.dot_general(gathered, full_projection, (((1,), (1,)), ((), ())), pref...  6.31 us
  transfers between devices with their start and end apart: 3, of which 3 were waited for; matrix products, arithmetic and copies ran while one was open for 8% of the time, Pallas kernels for 0%

commit v1 on v0

--- a/solution.py
+++ b/solution.py
@@ -35,7 +35,14 @@
         "hqk,khd->qhd", probs_low, value_heads, preferred_element_type=jnp.float32
     )
     attended = attended.astype(jnp.bfloat16).reshape(row_count, width)
-    full_projection = lax.all_gather(projection, "dp", axis=1, tiled=True)
+    devices = lax.axis_size("dp")
+    right = [(i, (i + 1) % devices) for i in range(devices)]
+    parts = [projection]
+    for hop in range(1, devices):
+        parts = [lax.ppermute(parts[0], "dp", right), *parts]
+    out = jnp.concatenate(parts, axis=1)
+    offset = (lax.axis_index("dp") + 1) * parts[-1].shape[1]
+    full_projection = jnp.roll(out, offset, axis=1)
     gathered = lax.all_gather(upstream, "tensor", axis=0, tiled=True)
     out_total = lax.dot_general(
         gathered, full_projection, (((1,), (1,)), ((), ())), preferred_element_type=jnp.float32

time: 227 us -> 207 us (0.912)
  waiting for transfers between devices: 192 us -> 170 us
    all_gather x1 -> x0, waiting for transfers between devices: 15.8 us -> none  [shards(): full_projection = lax.all_gather(projection, 'dp', axis=1, tiled=True)]
    ppermute x0 -> x3, waiting for transfers between devices: none -> 15.1 us  [shards(): parts = [lax.ppermute(parts[0], 'dp', right), *parts]]
    all_gather x1, waiting for transfers between devices: 151 us -> 136 us  [shards(): gathered = lax.all_gather(upstream, 'tensor', axis=0, tiled=True)]
    reduce_scatter x1, waiting for transfers between devices: 23.7 us -> 17.9 us  [shards(): lax.psum_scatter(partial_grad.astype(jnp.bfloat16), 'dp', scatter_dimensi...]
  transfers between devices with their start and end apart: 3 -> 5, of which waited for: 3 -> 4; matrix products, arithmetic and copies ran while one was open for 8% -> 9% of each run, Pallas kernels for 0% -> 0%
where the time goes in v1:
time: 207 us
  waiting for transfers between devices  170 us (82%)
  matrix products  17.2 us (8%)
  between operations  14.2 us (7%)
  other arithmetic  3.51 us (2%)
    all_gather x1, waiting for transfers between devices, shards(): gathered = lax.all_gather(upstream, 'tensor', axis=0, tiled=True)  136 us
    reduce_scatter x1, waiting for transfers between devices, shards(): lax.psum_scatter(partial_grad.astype(jnp.bfloat16), 'dp', scatter_dimensi...  17.9 us
    ppermute x3, waiting for transfers between devices, shards(): parts = [lax.ppermute(parts[0], 'dp', right), *parts]  15.1 us
    dot_general x1, matrix products, shards(): lax.dot_general(gathered, full_projection, (((1,), (1,)), ((), ())), pref...  6.66 us
    dot_general x1, matrix products, shards(): lax.dot_general(attended, gathered, (((0,), (0,)), ((), ())), preferred_e...  6.57 us
  transfers between devices with their start and end apart: 5, of which 4 were waited for; matrix products, arithmetic and copies ran while one was open for 9% of the time, Pallas kernels for 0%

profile of v1, /device:TPU:0, one launch (start us, length us, event | category | flops | bytes accessed | tf_op | source)
XLA Modules:
  0.0 207.0 jit_solution(1062112834928038333)
XLA Ops:
  7.2 0.0 all-gather.2.cloned.1.call-start
  7.2 0.7 all-gather.2.cloned.1.call-update
  7.9 0.0 reduce-scatter.2.cloned.1.call-start
  8.0 0.5 collective-permute-start
  8.5 0.8 reduce-window.8
  9.3 8.2 %collective-permute-done = bf16[128,2048]{1,0:T(8,128)(2,1)S(1)} collective-permute-done((bf16[128,2048]{1,0:T(8,128)(2,1)}, bf16[128,2048]{1,0:T(8,128)(2,1)S(1)}, u32[]{:S(2)}, u32[]{:S(2)}) %collective-permute-start) | collective-permute-done | bytes 524320 | tf_op jit(solution)/shard_map/ppermute | solution.py:42
  17.5 0.0 collective-permute-start.1
  17.5 0.1 convert_reduce_fusion
  17.6 1.3 fusion.17
  18.9 0.2 fusion.9
  19.1 7.0 %collective-permute-done.1 = bf16[128,2048]{1,0:T(8,128)(2,1)S(1)} collective-permute-done((bf16[128,2048]{1,0:T(8,128)(2,1)S(1)}, bf16[128,2048]{1,0:T(8,128)(2,1)S(1)}, u32[]{:S(2)}, u32[]{:S(2)}) %collective-permute-start.1) | collective-permute-done | bytes 524320 | tf_op jit(solution)/shard_map/ppermute | solution.py:42
  26.1 135.9 %all-gather.2.cloned.1.call-done = bf16[512,8192]{1,0:T(8,128)(2,1)} async-done(((bf16[128,8192]{1,0:T(8,128)(2,1)}), bf16[512,8192]{1,0:T(8,128)(2,1)}) %all-gather.2.cloned.1.call-update) | async-done | bytes 8388624 | tf_op jit(solution)/shard_map/all_gather | solution.py:46
  162.0 6.6 %convolution_convert_fusion = bf16[128,8192]{1,0:T(8,128)(2,1)} fusion(bf16[512,8192]{1,0:T(8,128)(2,1)} %all-gather.2.cloned.1.call-done, bf16[512,128]{1,0:T(8,128)(2,1)S(1)} %copy-done, f32[512,512]{0,1:T(8,128)S(1)} %get-tuple-element.13, f32[512]{0:T(512)S(1)} %fusion.9, f32[512]{0:T(512)S(1)} %get-tuple-element.12), kind=kOutput, calls=%fused_computation | convolution fusion | flops 1142751232 | bytes 11669504 | tf_op jit(solution)/shard_map/dot_general | solution.py:50
  168.5 0.0 reduce-scatter.2.cloned.1.call-update
  168.7 0.8 copy-done.1
  169.8 6.7 %fusion.3 = bf16[128,512]{1,0:T(8,128)(2,1)S(1)} fusion(bf16[512,8192]{1,0:T(8,128)(2,1)} %all-gather.2.cloned.1.call-done, bf16[128,16384]{1,0:T(8,128)(2,1)S(1)} %constant_dynamic-update-slice_fusion, s32[]{:T(128)S(6)} %select_n.20), kind=kOutput, calls=%fused_computation.9 | convolution fusion | flops 1073807360 | bytes 10616836 | tf_op jit(solution)/shard_map/dot_general | solution.py:47
  176.5 0.3 fusion.6
  176.9 0.8 copy.11
  177.6 0.3 multiply_reduce_fusion
  177.9 0.3 multiply_convert_fusion
  178.2 1.0 convolution_convert_fusion.3
  179.2 1.0 convolution_convert_fusion.4
  180.2 17.9 %reduce-scatter.2.cloned.1.call-done = bf16[128,2048]{1,0:T(8,128)(2,1)} async-done(((bf16[128,8192]{1,0:T(8,128)(2,1)}), bf16[128,2048]{1,0:T(8,128)(2,1)}) %reduce-scatter.2.cloned.1.call-update) | async-done | bytes 524304 | tf_op jit(solution)/shard_map/reduce_scatter | solution.py:53
  198.1 2.1 %convert_element_type.59 = f32[128,2048]{1,0:T(8,128)} convert(bf16[128,2048]{1,0:T(8,128)(2,1)} %reduce-scatter.2.cloned.1.call-done) | non-fusion elementwise | flops 262144 | bytes 1572864 | tf_op jit(solution)/shard_map/convert_element_type | solution.py:55
  (17 shorter events, 0.3 us)
Async XLA Ops:
  7.2 154.8 %copy-start = (bf16[512,128]{1,0:T(8,128)(2,1)S(1)}, bf16[512,128]{1,0:T(8,128)(2,1)}, u32[]{:S(2)}) copy-start(bf16[512,128]{1,0:T(8,128)(2,1)} %param.8) | copy-start | bytes 393220
  7.2 154.8 %all-gather.2.cloned.1.call-start = ((), (), s32[]{:S(2)}) async-start(), calls=%async_computation.1 | async-start | bytes 10485760 | tf_op jit(solution)/shard_map/all_gather | solution.py:46
  7.9 190.2 %reduce-scatter.2.cloned.1.call-start = ((), (), s32[]{:S(2)}) async-start(), calls=%async_computation.2 | async-start | bytes 2621440 | tf_op jit(solution)/shard_map/reduce_scatter | solution.py:53
  8.0 9.5 %collective-permute-start = (bf16[128,2048]{1,0:T(8,128)(2,1)}, bf16[128,2048]{1,0:T(8,128)(2,1)S(1)}, u32[]{:S(2)}, u32[]{:S(2)}) collective-permute-start(bf16[128,2048]{1,0:T(8,128)(2,1)} %param.10), channel_id=1, source_target_pairs={{0,4},{4,8},{8,12},{12,0},{1,5},{5,9},{9,13},{13,1},{2,6},{6,10},{... | collective-permute-start | bytes 1572872 | tf_op jit(solution)/shard_map/ppermute | solution.py:42
  17.5 8.6 %collective-permute-start.1 = (bf16[128,2048]{1,0:T(8,128)(2,1)S(1)}, bf16[128,2048]{1,0:T(8,128)(2,1)S(1)}, u32[]{:S(2)}, u32[]{:S(2)}) collective-permute-start(bf16[128,2048]{1,0:T(8,128)(2,1)S(1)} %collective-permute-done), channel_id=1, source_target_pairs={{0,4},{4,8},{8,12},{12,0},{1,5},{5,9},{9,13},{13,1},{2,6},{6,10},{... | collective-permute-start | bytes 1572872 | tf_op jit(solution)/shard_map/ppermute | solution.py:42
  26.1 142.5 %collective-permute-start.2 = (bf16[128,2048]{1,0:T(8,128)(2,1)S(1)}, bf16[128,2048]{1,0:T(8,128)(2,1)S(1)}, u32[]{:S(2)}, u32[]{:S(2)}) collective-permute-start(bf16[128,2048]{1,0:T(8,128)(2,1)S(1)} %collective-permute-done.1), channel_id=1, source_target_pairs={{0,4},{4,8},{8,12},{12,0},{1,5},{5,9},{9,13},{13,1},{2,6},{6,10},{... | collective-permute-start | bytes 1572872 | tf_op jit(solution)/shard_map/ppermute | solution.py:42
  168.5 1.0 copy-start.1
  176.8 1.4 copy-start.2
  176.8 2.4 %copy-start.3 = (bf16[512,128]{1,0:T(8,128)(2,1)S(1)}, bf16[512,128]{1,0:T(8,128)(2,1)}, u32[]{:S(2)}) copy-start(bf16[512,128]{1,0:T(8,128)(2,1)} %param.7) | copy-start | bytes 393220
Sparse Core Ops, SparseCore 0:
  9.6 152.3 all-gather.1
  168.7 29.3 reduce-scatter.1
